TPU v7x, 32 devices: a whole 2x2x4 slice. The times are simulated.
32 devices in a mesh: wide: 8 (over z, y), narrow: 4 (over x, core).
Axes of the slice: x: 2, y: 2, z: 4, core: 2. Of those that a mesh axis runs over, the one named last changes fastest.
Arguments:
- left_edge: bfloat16 [448, 49, 448], P('wide', None, 'narrow'), may hold values from -40 to 40
- corner: bfloat16 [448, 448], P('narrow'), may hold values from -0.25 to 0.25
- right_edge: bfloat16 [448, 49, 448], P('wide', None, 'narrow'), may hold values from -0.25 to 0.25
- single_layer: bfloat16 [2, 2401], replicated, may hold values from -0.71875 to 0.71875
- warm_basis: bfloat16 [49, 448, 448], P(None, 'narrow', 'wide'), may hold values from -0.0390625 to 0.0390625
Outputs:
- new_basis: float32 [448, 49, 448], P('wide', None, 'narrow')
- r_factor: float32 [448, 448], replicated
All inputs are finite; a program needn't handle non-finite values.
Results may differ from a plain program's by a relative error of at most 0.014.
Values may be sent and summed in bfloat16 or wider, within the bound.
No kernel may reach another device: no remote copies, remote signals or barrier semaphores. Data moves between devices by JAX's collectives and lax.ppermute only.
A program may use at most 192 MiB of HBM per device.

v0:
```python
import jax
import jax.numpy as jnp
from jax import lax
from jax.sharding import PartitionSpec as P

BOND = 7


def on_device(left_edge, corner, right_edge, single_layer, warm_basis):
    local_rows = left_edge.shape[0]
    square = left_edge.shape[1]
    breadth = corner.shape[1]
    local_cols = right_edge.shape[2]
    partial_value = jnp.dot(
        left_edge.reshape(local_rows * square, left_edge.shape[2]),
        corner,
        preferred_element_type=jnp.float32,
    )
    half_left = lax.psum(partial_value, "narrow").astype(jnp.bfloat16)
    layer = single_layer.astype(jnp.float32).reshape(single_layer.shape[0], BOND, BOND, BOND, BOND)
    piece = lax.all_gather(right_edge, "wide", axis=0, tiled=True)
    strip_sum = jnp.dot(
        half_left,
        piece.reshape(piece.shape[0], square * local_cols),
        preferred_element_type=jnp.float32,
    )
    strip = (
        strip_sum.astype(jnp.bfloat16)
        .astype(jnp.float32)
        .reshape(local_rows, BOND, BOND, BOND, BOND, local_cols)
    )
    ket_layer = jnp.einsum("iuvlmj,suldr->ivmsdrj", strip, layer)
    enlarged = jnp.einsum("ivmsdrj,svmew->iderwj", ket_layer, layer)
    enlarged = enlarged.astype(jnp.bfloat16).reshape(local_rows * square, square * local_cols)
    piece = lax.all_gather(warm_basis, "wide", axis=2, tiled=True)
    partial_rows = jnp.dot(
        enlarged,
        piece.reshape(square * local_cols, piece.shape[2]),
        preferred_element_type=jnp.float32,
    )
    projected = lax.psum(partial_rows.astype(jnp.bfloat16), "narrow").astype(jnp.float32)
    all_rows = breadth * square
    own_index = lax.axis_index("narrow")
    gram_term = (
        jnp.dot(
            projected.T,
            projected,
            precision=lax.Precision.HIGHEST,
            preferred_element_type=jnp.float32,
        )
        / all_rows
    )
    gram = lax.psum(gram_term, "wide")
    lower = jnp.linalg.cholesky(gram)
    solved = lax.linalg.triangular_solve(lower, projected.T, left_side=True, lower=True)
    own_solved = lax.dynamic_slice_in_dim(solved, own_index * local_cols, local_cols, 0)
    new_basis = own_solved.T.reshape(local_rows, square, local_cols)
    return (new_basis, lower.T)


def solution(mesh):
    placed = (
        P("wide", None, "narrow"),
        P("narrow", None),
        P("wide", None, "narrow"),
        P(),
        P(None, "narrow", "wide"),
    )
    return jax.shard_map(
        on_device,
        mesh=mesh,
        in_specs=placed,
        out_specs=(P("wide", None, "narrow"), P()),
        check_vma=False,
    )
```

profile of v0, /device:TPU:0, one launch (start us, length us, event | category | flops | bytes accessed | tf_op | source)
XLA Modules:
  0.0 761.6 jit_solution(3121338594406813243)
XLA Ops:
  7.2 0.7 all-gather.3.cloned.1.call-update
  8.0 0.7 all-gather.5.cloned.1.call-update
  8.7 0.9 reshape.89
  9.7 0.9 reshape.65
  10.6 1.2 copy.13
  12.1 3.4 fusion.53
  15.5 103.2 %all-reduce.10 = bf16[2744,448]{1,0:T(8,128)(2,1)S(1)} all-reduce(f32[2744,448]{1,0:T(8,128)} %fusion.53), channel_id=1, replica_groups=mesh['wide'=8,'narrow'=4] {'narrow'}, use_global_device_ids=true, to_apply=%region_0.0 | all-reduce | flops 1229312 | bytes 7375872 | tf_op jit(solution)/shard_map/psum | solution.py:19
  118.7 8.6 %copy.14 = bf16[448,49,112]{0,2,1:T(8,128)(2,1)} copy(bf16[448,49,112]{2,0,1:T(8,128)(2,1)} %all-gather.3.cloned.1.call-done) | data formatting | bytes 9834496 | tf_op jit(solution)/shard_map/all_gather | solution.py:21
  127.3 22.5 %convolution_convert_fusion = bf16[2744,5488]{1,0:T(8,128)(2,1)} fusion(bf16[448,5488]{0,1:T(8,128)(2,1)} %bitcast.86, bf16[2744,448]{1,0:T(8,128)(2,1)S(1)} %all-reduce.10), kind=kOutput, calls=%fused_computation.9 | convolution fusion | flops 13507987456 | bytes 37494016 | tf_op jit(solution)/shard_map/dot_general | solution.py:22
  149.8 68.2 %reshape.88 = bf16[56,7,7,7,7,112,1,1]{5,4,3,2,1,0,6,7:T(8,128)(2,1)} reshape(bf16[2744,5488]{1,0:T(8,128)(2,1)} %convolution_convert_fusion) | data formatting | bytes 60236288 | tf_op jit(solution)/shard_map/reshape | solution.py:30
  218.0 42.5 %fusion.4 = bf16[56,7,7,112,2,7,7,1]{3,6,7,5,4,2,1,0:T(8,128)(2,1)} fusion(bf16[56,7,7,7,7,112,1,1]{5,4,3,2,1,0,6,7:T(8,128)(2,1)} %reshape.88, bf16[2,7,7,7,7,1,1,1]{4,3,2,1,0,5,6,7:T(8,128)(2,1)S(1)} %reshape.89), kind=kOutput, calls=%fused_computation.7 | convolution fusion | flops 2951578112 | bytes 90364032 | tf_op jit(solution)/shard_map/iuvlmj,suldr->ivmsdrj/dot_general | solution.py:32
  260.6 64.9 %fusion.3 = bf16[56,7,7,7,7,112]{5,4,2,3,1,0:T(8,128)(2,1)} fusion(bf16[56,7,7,112,2,7,7,1]{3,6,7,5,4,2,1,0:T(8,128)(2,1)} %fusion.4, bf16[2,7,7,7,7,1,1,1]{4,3,2,1,0,7,6,5:T(8,128)(2,1)S(1)} %bitcast.89), kind=kOutput, calls=%fused_computation.6 | convolution fusion | flops 2951578112 | bytes 90364032 | tf_op jit(solution)/shard_map/ivmsdrj,svmew->iderwj/dot_general | solution.py:33
  325.5 25.9 %copy.16 = bf16[56,7,7,7,7,112]{5,4,3,2,1,0:T(8,128)(2,1)} copy(bf16[56,7,7,7,7,112]{5,4,2,3,1,0:T(8,128)(2,1)} %fusion.3) | data formatting | bytes 60236288 | tf_op jit(solution)/shard_map/convert_element_type | solution.py:34
  351.4 55.3 %reshape.66 = bf16[2744,5488]{1,0:T(8,128)(2,1)} reshape(bf16[56,7,7,7,7,112]{5,4,3,2,1,0:T(8,128)(2,1)} %copy.16) | data formatting | bytes 60236288 | tf_op jit(solution)/shard_map/reshape | solution.py:34
  406.7 8.5 %copy.17 = bf16[49,112,448]{2,1,0:T(8,128)(2,1)} copy(bf16[49,112,448]{1,2,0:T(8,128)(2,1)} %all-gather.5.cloned.1.call-done) | data formatting | bytes 9834496 | tf_op jit(solution)/shard_map/all_gather | solution.py:35
  415.3 22.7 %convolution_convert_fusion.1 = bf16[2744,448]{0,1:T(8,128)(2,1)} fusion(bf16[2744,5488]{1,0:T(8,128)(2,1)} %reshape.66, bf16[5488,448]{1,0:T(8,128)(2,1)} %bitcast.87), kind=kOutput, calls=%fused_computation.14 | convolution fusion | flops 13494157312 | bytes 37494016 | tf_op jit(solution)/shard_map/dot_general | solution.py:36
  438.5 0.6 pad_convert_fusion
  439.1 57.9 %all-reduce.7.cloned.1.call-done = bf16[2744,448]{0,1:T(8,128)(2,1)} async-done(((bf16[2744,448]{0,1:T(8,128)(2,1)}), bf16[2744,448]{0,1:T(8,128)(2,1)}) %all-reduce.7.cloned.1.call-update) | async-done | bytes 2458640 | tf_op jit(solution)/shard_map/psum | solution.py:41
  497.1 5.0 convolution_multiply_fusion
  502.1 2.6 bitcast_convert_fusion.1
  504.7 74.6 %all-reduce.9.cloned.1.call-done = f32[448,448]{0,1:T(8,128)} async-done(((f32[448,448]{0,1:T(8,128)}), f32[448,448]{0,1:T(8,128)}) %all-reduce.9.cloned.1.call-update) | async-done | bytes 802832 | tf_op jit(solution)/shard_map/psum | solution.py:53
  579.3 1.5 copy.19
  580.8 1.4 fusion.25
  582.1 0.9 copy-done.5
  583.1 11.7 %cholesky.105 = f32[128,128]{1,0:T(8,128)S(1)} custom-call(f32[128,128]{1,0:T(8,128)S(1)} %cholesky.272), custom_call_target="Cholesky" | custom-call | tf_op jit(solution)/shard_map/jit(cholesky)/cholesky | solution.py:54
  594.8 10.4 %custom-call.30 = f32[1,128,128]{1,2,0:T(8,128)} custom-call(f32[1,128,128]{2,1,0:T(8,128)S(1)} %get-tuple-element.33), custom_call_target="InvertDiagBlocksLowerTriangular" | custom-call | tf_op jit(solution)/shard_map/jit(cholesky)/cholesky | solution.py:54
  605.4 1.2 constant_dynamic-update-slice_fusion
  606.6 1.2 convolution_subtract_fusion.2
  607.8 0.7 copy-done.6
  608.5 0.6 cholesky.276
  609.1 12.5 %cholesky.219 = f32[128,128]{1,0:T(8,128)S(1)} custom-call(f32[128,128]{1,0:T(8,128)} %cholesky.276), custom_call_target="Cholesky" | custom-call | tf_op jit(solution)/shard_map/jit(cholesky)/cholesky | solution.py:54
  621.7 0.8 select_reduce_fusion.1
  622.5 10.6 %custom-call.31 = f32[1,128,128]{1,2,0:T(8,128)S(1)} custom-call(f32[1,128,128]{2,1,0:T(8,128)} %get-tuple-element.30), custom_call_target="InvertDiagBlocksLowerTriangular" | custom-call | tf_op jit(solution)/shard_map/jit(cholesky)/cholesky | solution.py:54
  633.1 1.1 convolution_dynamic-update-slice_fusion
  634.3 1.2 convolution_subtract_fusion.3
  635.5 0.6 cholesky.281
  636.1 13.2 %cholesky.240 = f32[128,128]{1,0:T(8,128)} custom-call(f32[128,128]{1,0:T(8,128)} %cholesky.281), custom_call_target="Cholesky" | custom-call | tf_op jit(solution)/shard_map/jit(cholesky)/cholesky | solution.py:54
  649.3 1.5 select_reduce_fusion
  650.8 0.7 compare_reduce_fusion.1
  651.4 11.3 %custom-call.32 = f32[1,128,128]{1,2,0:T(8,128)} custom-call(f32[1,128,128]{2,1,0:T(8,128)} %get-tuple-element.27), custom_call_target="InvertDiagBlocksLowerTriangular" | custom-call | tf_op jit(solution)/shard_map/jit(cholesky)/cholesky | solution.py:54
  662.7 1.0 convolution_dynamic-update-slice_fusion.1
  663.7 1.0 convolution_subtract_fusion.4
  664.8 6.5 cholesky.260
  671.3 0.8 select_reduce_fusion.3
  672.0 0.7 compare_reduce_fusion
  672.8 0.6 compare_reduce_fusion.2
  676.0 1.2 fusion.27
  677.2 0.9 copy-done.4
  678.1 10.6 %while.1 = (s32[]{:T(128)}, f32[448,448]{1,0:T(8,128)}, s32[3,2]{0,1:T(2,128)S(1)}, f32[3,128,128]{2,1,0:T(8,128)}, s32[]{:T(128)}) while((s32[]{:T(128)}, f32[448,448]{1,0:T(8,128)}, s32[3,2]{0,1:T(2,128)S(1)}, f32[3,128,128]{2,1,0:T(8,128)}, s32[]{:T(128)}) %tuple.45), condition=%wide.while_cond, body=%wide.while_body.sunk | while | flops 2 | bytes 132705 | solution.py:55
  678.8 2.9 bitcast_dynamic-update-slice_fusion.2
  682.3 2.9 bitcast_dynamic-update-slice_fusion.2
  685.8 2.9 bitcast_dynamic-update-slice_fusion.2
  688.8 0.9 pad_maximum_fusion
  689.8 39.5 %custom-call.33 = f32[4,128,128]{1,2,0:T(8,128)S(1)} custom-call(f32[4,128,128]{2,1,0:T(8,128)S(1)} %pad_maximum_fusion), custom_call_target="InvertDiagBlocksLowerTriangular" | custom-call | tf_op jit(solution)/shard_map/triangular_solve | solution.py:55
  729.3 1.3 fusion.28
  730.6 2.8 convolution_subtract_fusion.1
  733.4 2.5 fusion.42
  735.9 4.1 convolution_subtract_fusion
  740.0 2.5 fusion.40
  742.5 5.4 fusion.14
  747.9 2.4 fusion.48
  750.4 1.5 fusion.24
  752.0 1.3 copy.21
  753.4 1.2 copy.22
  (38 shorter events, 3.3 us)
Async XLA Ops:
  7.2 4.9 copy-start
  7.2 111.5 %all-gather.3.cloned.1.call-start = ((), (), s32[]{:S(2)}) async-start(), calls=%async_computation | async-start | bytes 6322176 | tf_op jit(solution)/shard_map/all_gather | solution.py:21
  7.9 398.8 %all-gather.5.cloned.1.call-start = ((), (), s32[]{:S(2)}) async-start(), calls=%async_computation.1 | async-start | bytes 6322176 | tf_op jit(solution)/shard_map/all_gather | solution.py:35
  8.7 488.4 %all-reduce.7.cloned.1.call-start = ((), (), s32[]{:S(2)}) async-start(), calls=%async_computation.2 | async-start | bytes 5046272 | tf_op jit(solution)/shard_map/psum | solution.py:41
  438.0 141.3 %all-reduce.9.cloned.1.call-start = ((), (), s32[]{:S(2)}) async-start(), calls=%async_computation.3 | async-start | bytes 1835008 | tf_op jit(solution)/shard_map/psum | solution.py:53
  497.1 5.1 copy-start.2
  582.1 0.9 copy-start.5
  607.8 0.7 copy-start.6
  663.7 25.0 %copy-start.7 = (f32[128,64]{1,0:T(8,128)S(1)}, f32[128,64]{1,0:T(8,128)}, u32[]{:S(2)}) copy-start(f32[128,64]{1,0:T(8,128)} %pad_convert_fusion) | copy-start | bytes 98308
  677.2 0.9 copy-start.4
  751.9 2.7 copy-start.1
  752.0 1.4 copy-start.3
Sparse Core Ops, SparseCore 0:
  10.1 92.7 all-gather.2
  105.0 88.7 all-gather.4
  438.1 58.9 all-reduce.6
  502.2 76.9 all-reduce.8
where the time goes:
time: 774 us; the launch traced here: 762 us
  local copies, waits for them, and re-layouts  189 us (24%)
  matrix products  189 us (24%)
  waiting for transfers between devices  134 us (17%)
  other arithmetic  129 us (17%)
  blocking collectives  103 us (13%)
  between operations  17.1 us (2%)
    psum x1, blocking collectives, on_device(): half_left = lax.psum(partial_value, 'narrow').astype(jnp.bfloat16)  103 us
    another operation x14, other arithmetic, on_device(): lower = jnp.linalg.cholesky(gram)  81.4 us
    psum x1, waiting for transfers between devices, on_device(): gram = lax.psum(gram_term, 'wide')  74.6 us
    reshape x1, local copies, waits for them, and re-layouts, on_device(): strip = strip_sum.astype(jnp.bfloat16).astype(jnp.float32).reshape(local_...  68.2 us
    dot_general x1, matrix products, on_device(): enlarged = jnp.einsum('ivmsdrj,svmew->iderwj', ket_layer, layer)  64.9 us
    psum x1, waiting for transfers between devices, on_device(): lax.psum(partial_rows.astype(jnp.bfloat16), 'narrow').astype(jnp.float32)  57.9 us
    reshape x1, local copies, waits for them, and re-layouts, on_device(): enlarged.astype(jnp.bfloat16)  55.3 us
    dot_general x1, matrix products, on_device(): ket_layer = jnp.einsum('iuvlmj,suldr->ivmsdrj', strip, layer)  42.5 us
  transfers between devices with their start and end apart: 4, of which 2 were waited for; matrix products, arithmetic and copies ran while one was open for 39% of the time, Pallas kernels for 0%

commit v1 on v0

--- a/solution.py
+++ b/solution.py
@@ -4,6 +4,12 @@
 from jax.sharding import PartitionSpec as P
 
 BOND = 7
+
+
+def add_all(x, mesh_axis):
+    shards = lax.all_gather(x, mesh_axis, axis=0, tiled=False)
+    summed = shards.sum(axis=0)
+    return summed
 
 
 def on_device(left_edge, corner, right_edge, single_layer, warm_basis):
@@ -16,7 +22,7 @@
         corner,
         preferred_element_type=jnp.float32,
     )
-    half_left = lax.psum(partial_value, "narrow").astype(jnp.bfloat16)
+    half_left = add_all(partial_value, "narrow").astype(jnp.bfloat16)
     layer = single_layer.astype(jnp.float32).reshape(single_layer.shape[0], BOND, BOND, BOND, BOND)
     piece = lax.all_gather(right_edge, "wide", axis=0, tiled=True)
     strip_sum = jnp.dot(

time: 774 us -> 968 us (1.25)
  waiting for transfers between devices: 134 us -> 423 us
  blocking collectives: 103 us -> 0 us
    all_gather x0 -> x1, waiting for transfers between devices: none -> 119 us  [add_all(): shards = lax.all_gather(x, mesh_axis, axis=0, tiled=False)]
    psum x1 -> x0, blocking collectives: 103 us -> none  [on_device(): half_left = lax.psum(partial_value, 'narrow').astype(jnp.bfloat16)]
    all_gather x1, waiting for transfers between devices: 0.02 us -> 88.7 us  [on_device(): piece = lax.all_gather(right_edge, 'wide', axis=0, tiled=True)]
    all_gather x1, waiting for transfers between devices: 0.01 us -> 82.3 us  [on_device(): piece = lax.all_gather(warm_basis, 'wide', axis=2, tiled=True)]
  transfers between devices with their start and end apart: 4 -> 5, of which waited for: 2 -> 5; matrix products, arithmetic and copies ran while one was open for 39% -> 3% of each run, Pallas kernels for 0% -> 0%
where the time goes in v1:
time: 968 us; the launch traced here: 955 us
  waiting for transfers between devices  423 us (44%)
  matrix products  189 us (20%)
  local copies, waits for them, and re-layouts  187 us (19%)
  other arithmetic  138 us (14%)
  between operations  17 us (2%)
    all_gather x1, waiting for transfers between devices, add_all(): shards = lax.all_gather(x, mesh_axis, axis=0, tiled=False)  119 us
    all_gather x1, waiting for transfers between devices, on_device(): piece = lax.all_gather(right_edge, 'wide', axis=0, tiled=True)  88.7 us
    all_gather x1, waiting for transfers between devices, on_device(): piece = lax.all_gather(warm_basis, 'wide', axis=2, tiled=True)  82.3 us
    another operation x14, other arithmetic, on_device(): lower = jnp.linalg.cholesky(gram)  82.1 us
    psum x1, waiting for transfers between devices, on_device(): gram = lax.psum(gram_term, 'wide')  74.5 us
    reshape x1, local copies, waits for them, and re-layouts, on_device(): strip = strip_sum.astype(jnp.bfloat16).astype(jnp.float32).reshape(local_...  68.2 us
    dot_general x1, matrix products, on_device(): enlarged = jnp.einsum('ivmsdrj,svmew->iderwj', ket_layer, layer)  64.9 us
    psum x1, waiting for transfers between devices, on_device(): lax.psum(partial_rows.astype(jnp.bfloat16), 'narrow').astype(jnp.float32)  57.3 us
  transfers between devices with their start and end apart: 5, of which 5 were waited for; matrix products, arithmetic and copies ran while one was open for 3% of the time, Pallas kernels for 0%

profile of v1, /device:TPU:0, one launch (start us, length us, event | category | flops | bytes accessed | tf_op | source)
XLA Modules:
  0.0 954.7 jit_solution(7898684140776945155)
XLA Ops:
  7.2 0.7 all-gather.6.cloned.1.call-update
  8.0 0.7 all-gather.8.cloned.1.call-update
  8.7 1.2 copy.23
  10.2 3.1 convolution_bitcast_fusion.1
  14.2 88.7 %all-gather.6.cloned.1.call-done = bf16[448,49,112]{2,0,1:T(8,128)(2,1)} async-done(((bf16[56,49,112]{2,0,1:T(8,128)(2,1)}), bf16[448,49,112]{2,0,1:T(8,128)(2,1)}) %all-gather.6.cloned.1.call-update) | async-done | bytes 4917264 | tf_op jit(solution)/shard_map/all_gather | solution.py:27
  102.9 8.6 copy.24
  111.4 82.3 %all-gather.8.cloned.1.call-done = bf16[49,112,448]{1,2,0:T(8,128)(2,1)} async-done(((bf16[49,112,56]{1,2,0:T(8,128)(2,1)}), bf16[49,112,448]{1,2,0:T(8,128)(2,1)}) %all-gather.8.cloned.1.call-update) | async-done | bytes 4917264 | tf_op jit(solution)/shard_map/all_gather | solution.py:41
  193.8 8.6 copy.30
  202.4 118.9 %all-gather.10.cloned.1.call-done = f32[4,2744,448]{1,2,0:T(8,128)} async-done(((f32[1,2744,448]{1,2,0:T(8,128)}), f32[4,2744,448]{1,2,0:T(8,128)}) %all-gather.10.cloned.1.call-update) | async-done | bytes 19669008 | tf_op jit(solution)/shard_map/all_gather | solution.py:10
  321.3 8.0 reduce_sum.9
  329.3 22.6 %convolution_convert_fusion = bf16[2744,5488]{1,0:T(8,128)(2,1)} fusion(bf16[448,5488]{0,1:T(8,128)(2,1)} %bitcast.88, bf16[2744,448]{0,1:T(8,128)(2,1)S(1)} %reduce_sum.9), kind=kOutput, calls=%fused_computation.8 | convolution fusion | flops 13507987456 | bytes 37494016 | tf_op jit(solution)/shard_map/dot_general | solution.py:28
  351.9 68.2 %reshape.64 = bf16[56,7,7,7,7,112]{5,4,3,2,1,0:T(8,128)(2,1)} reshape(bf16[2744,5488]{1,0:T(8,128)(2,1)} %convolution_convert_fusion) | data formatting | bytes 60236288 | tf_op jit(solution)/shard_map/reshape | solution.py:36
  420.1 42.5 %convolution_bitcast_fusion = bf16[56,7,7,2,7,7,112,1]{6,5,4,3,2,1,0,7:T(8,128)(2,1)} fusion(bf16[56,7,7,7,7,112,1,1]{5,4,3,2,1,0,7,6:T(8,128)(2,1)} %bitcast.86, bf16[2,7,7,7,7,1,1,1]{4,3,2,1,0,7,6,5:T(8,128)(2,1)S(1)} %bitcast.90), kind=kOutput, calls=%fused_computation.5 | convolution fusion | flops 2951578112 | bytes 90364032 | tf_op jit(solution)/shard_map/iuvlmj,suldr->ivmsdrj/dot_general | solution.py:38
  462.7 64.9 %fusion.2 = bf16[56,7,7,7,7,112]{5,4,2,3,1,0:T(8,128)(2,1)} fusion(bf16[56,7,7,2,7,7,112,1]{6,5,4,3,2,1,0,7:T(8,128)(2,1)} %convolution_bitcast_fusion, bf16[2,7,7,7,7,1,1,1]{4,3,2,1,0,7,6,5:T(8,128)(2,1)S(1)} %bitcast.91), kind=kOutput, calls=%fused_computation.6 | convolution fusion | flops 2951578112 | bytes 90364032 | tf_op jit(solution)/shard_map/ivmsdrj,svmew->iderwj/dot_general | solution.py:39
  527.6 26.0 %copy.29 = bf16[56,7,7,7,7,112]{5,4,3,2,1,0:T(8,128)(2,1)} copy(bf16[56,7,7,7,7,112]{5,4,2,3,1,0:T(8,128)(2,1)} %fusion.2) | data formatting | bytes 60236288 | tf_op jit(solution)/shard_map/convert_element_type | solution.py:40
  553.5 55.3 %reshape.66 = bf16[2744,5488]{1,0:T(8,128)(2,1)} reshape(bf16[56,7,7,7,7,112]{5,4,3,2,1,0:T(8,128)(2,1)} %copy.29) | data formatting | bytes 60236288 | tf_op jit(solution)/shard_map/reshape | solution.py:40
  608.8 22.6 %convolution_convert_fusion.1 = bf16[2744,448]{0,1:T(8,128)(2,1)} fusion(bf16[2744,5488]{1,0:T(8,128)(2,1)} %reshape.66, bf16[5488,448]{1,0:T(8,128)(2,1)} %bitcast.87), kind=kOutput, calls=%fused_computation.14 | convolution fusion | flops 13494157312 | bytes 37494016 | tf_op jit(solution)/shard_map/dot_general | solution.py:42
  632.0 0.6 pad_convert_fusion
  632.6 57.3 %all-reduce.6.cloned.1.call-done = bf16[2744,448]{0,1:T(8,128)(2,1)} async-done(((bf16[2744,448]{0,1:T(8,128)(2,1)}), bf16[2744,448]{0,1:T(8,128)(2,1)}) %all-reduce.6.cloned.1.call-update) | async-done | bytes 2458640 | tf_op jit(solution)/shard_map/psum | solution.py:47
  690.0 5.0 convolution_multiply_fusion
  695.0 2.5 bitcast_convert_fusion.1
  697.6 74.5 %all-reduce.8.cloned.1.call-done = f32[448,448]{0,1:T(8,128)} async-done(((f32[448,448]{0,1:T(8,128)}), f32[448,448]{0,1:T(8,128)}) %all-reduce.8.cloned.1.call-update) | async-done | bytes 802832 | tf_op jit(solution)/shard_map/psum | solution.py:59
  772.1 1.5 copy.32
  773.6 1.4 fusion.23
  775.0 0.9 copy-done.5
  775.9 11.7 %cholesky.105 = f32[128,128]{1,0:T(8,128)S(1)} custom-call(f32[128,128]{1,0:T(8,128)S(1)} %cholesky.272), custom_call_target="Cholesky" | custom-call | tf_op jit(solution)/shard_map/jit(cholesky)/cholesky | solution.py:60
  787.6 0.7 select_reduce_fusion.2
  788.4 10.6 %custom-call.30 = f32[1,128,128]{1,2,0:T(8,128)S(1)} custom-call(f32[1,128,128]{2,1,0:T(8,128)} %get-tuple-element.35), custom_call_target="InvertDiagBlocksLowerTriangular" | custom-call | tf_op jit(solution)/shard_map/jit(cholesky)/cholesky | solution.py:60
  799.0 1.2 constant_dynamic-update-slice_fusion
  800.2 1.2 convolution_subtract_fusion.2
  801.5 0.7 copy-done.6
  802.8 12.5 %cholesky.219 = f32[128,128]{1,0:T(8,128)S(1)} custom-call(f32[128,128]{1,0:T(8,128)} %cholesky.276), custom_call_target="Cholesky" | custom-call | tf_op jit(solution)/shard_map/jit(cholesky)/cholesky | solution.py:60
  815.3 0.8 select_reduce_fusion.1
  816.1 10.6 %custom-call.31 = f32[1,128,128]{1,2,0:T(8,128)S(1)} custom-call(f32[1,128,128]{2,1,0:T(8,128)} %get-tuple-element.32), custom_call_target="InvertDiagBlocksLowerTriangular" | custom-call | tf_op jit(solution)/shard_map/jit(cholesky)/cholesky | solution.py:60
  826.8 1.1 convolution_dynamic-update-slice_fusion
  827.9 1.2 convolution_subtract_fusion.3
  829.1 0.6 cholesky.281
  829.8 13.2 %cholesky.240 = f32[128,128]{1,0:T(8,128)} custom-call(f32[128,128]{1,0:T(8,128)} %cholesky.281), custom_call_target="Cholesky" | custom-call | tf_op jit(solution)/shard_map/jit(cholesky)/cholesky | solution.py:60
  842.9 1.5 select_reduce_fusion
  844.4 0.7 compare_reduce_fusion.1
  845.1 11.3 %custom-call.32 = f32[1,128,128]{1,2,0:T(8,128)} custom-call(f32[1,128,128]{2,1,0:T(8,128)} %get-tuple-element.29), custom_call_target="InvertDiagBlocksLowerTriangular" | custom-call | tf_op jit(solution)/shard_map/jit(cholesky)/cholesky | solution.py:60
  856.4 1.0 convolution_dynamic-update-slice_fusion.1
  857.4 1.0 convolution_subtract_fusion.4
  858.5 6.5 cholesky.260
  864.9 0.8 select_reduce_fusion.3
  866.3 0.6 compare_reduce_fusion.2
  869.4 1.2 fusion.25
  870.6 0.9 copy-done.4
  871.5 10.3 %while.1 = (s32[]{:T(128)}, f32[448,448]{1,0:T(8,128)}, s32[3,2]{0,1:T(2,128)S(1)}, f32[3,128,128]{2,1,0:T(8,128)}, s32[]{:T(128)}) while((s32[]{:T(128)}, f32[448,448]{1,0:T(8,128)}, s32[3,2]{0,1:T(2,128)S(1)}, f32[3,128,128]{2,1,0:T(8,128)}, s32[]{:T(128)}) %tuple.48), condition=%wide.while_cond, body=%wide.while_body.sunk | while | flops 2 | bytes 132705 | solution.py:61
  872.1 2.8 bitcast_dynamic-update-slice_fusion.2
  875.6 2.8 bitcast_dynamic-update-slice_fusion.2
  879.0 2.8 bitcast_dynamic-update-slice_fusion.2
  881.9 0.9 pad_maximum_fusion
  882.9 39.5 %custom-call.33 = f32[4,128,128]{1,2,0:T(8,128)S(1)} custom-call(f32[4,128,128]{2,1,0:T(8,128)S(1)} %pad_maximum_fusion), custom_call_target="InvertDiagBlocksLowerTriangular" | custom-call | tf_op jit(solution)/shard_map/triangular_solve | solution.py:61
  922.4 1.3 fusion.26
  923.7 2.8 convolution_subtract_fusion.1
  926.5 2.5 fusion.40
  929.0 4.1 convolution_subtract_fusion
  933.2 2.5 fusion.38
  935.7 5.4 fusion.12
  941.1 2.4 fusion.46
  943.5 1.5 fusion.22
  945.2 1.3 copy.36
  946.5 1.2 copy.37
  (42 shorter events, 5.3 us)
Async XLA Ops:
  7.2 3.1 copy-start
  7.2 95.7 %all-gather.6.cloned.1.call-start = ((), (), s32[]{:S(2)}) async-start(), calls=%async_computation | async-start | bytes 6322176 | tf_op jit(solution)/shard_map/all_gather | solution.py:27
  7.9 185.9 %all-gather.8.cloned.1.call-start = ((), (), s32[]{:S(2)}) async-start(), calls=%async_computation.1 | async-start | bytes 6322176 | tf_op jit(solution)/shard_map/all_gather | solution.py:41
  8.7 312.7 %all-gather.10.cloned.1.call-start = ((), (), s32[]{:S(2)}) async-start(), calls=%async_computation.4 | async-start | bytes 25231360 | tf_op jit(solution)/shard_map/all_gather | solution.py:10
  13.3 0.7 copy-start.8
  13.3 676.7 %all-reduce.6.cloned.1.call-start = ((), (), s32[]{:S(2)}) async-start(), calls=%async_computation.2 | async-start | bytes 5046272 | tf_op jit(solution)/shard_map/psum | solution.py:47
  631.5 140.6 %all-reduce.8.cloned.1.call-start = ((), (), s32[]{:S(2)}) async-start(), calls=%async_computation.3 | async-start | bytes 1835008 | tf_op jit(solution)/shard_map/psum | solution.py:59
  690.0 5.1 copy-start.2
  775.0 0.9 copy-start.5
  801.5 0.7 copy-start.6
  857.4 24.4 %copy-start.7 = (f32[128,64]{1,0:T(8,128)S(1)}, f32[128,64]{1,0:T(8,128)}, u32[]{:S(2)}) copy-start(f32[128,64]{1,0:T(8,128)} %pad_convert_fusion) | copy-start | bytes 98308
  870.6 0.9 copy-start.4
  945.0 2.7 copy-start.1
  945.2 1.4 copy-start.3
Sparse Core Ops, SparseCore 0:
  10.1 92.7 all-gather.5
  105.0 88.7 all-gather.7
  195.4 125.9 all-gather.9
  631.6 58.2 all-reduce.5
  695.2 76.8 all-reduce.7
